TPU v7x, 32 devices: a whole 2x2x4 slice. The times are simulated.
32 devices in a mesh: row: 4 (over y, x), col: 8 (over z, core).
Axes of the slice: x: 2, y: 2, z: 4, core: 2. Of those that a mesh axis runs over, the one named last changes fastest.
Arguments:
- tokens: bfloat16 [512, 5120], P('row'), may hold values from -6 to 6
- expert_ids: int32 [512], replicated, may hold values from 0 to 7
- modality: int32 [512], replicated, may hold values from 0 to 1
- tile_counts: int32 [2, 8], replicated, may hold values from 1 to 4, as said below
- router: bfloat16 [5120, 8], P(None, 'col'), may hold values from -0.15625 to 0.15625
- w_gate: bfloat16 [8, 5120, 4096], P('col', None, 'row'), may hold values from -0.078125 to 0.078125
- w_up: bfloat16 [8, 5120, 4096], P('col', None, 'row'), may hold values from -0.078125 to 0.078125
- w_down: bfloat16 [8, 4096, 5120], P('col', 'row'), may hold values from -0.09375 to 0.09375
- shared_gate: bfloat16 [5120, 8192], P('row', 'col'), may hold values from -0.078125 to 0.078125
- shared_up: bfloat16 [5120, 8192], P('row', 'col'), may hold values from -0.078125 to 0.078125
- shared_down: bfloat16 [8192, 5120], P('col', 'row'), may hold values from -0.0625 to 0.0625
Outputs:
- mixed: bfloat16 [512, 5120], P('col', 'row')
Inputs may be any that keep to these rules, and one draw needn't show every extreme that they name: `tile_counts`: in every draw some expert's text segment has 4 tiles and at least 32 text tokens, and some expert's image segment has 4 tiles and at least 32 image tokens.
All inputs are finite; a program needn't handle non-finite values.
Results may differ from a plain program's by a relative error of at most 0.0052.
Values may be sent and summed in bfloat16 or wider, within the bound.
No kernel may reach another device: no remote copies, remote signals or barrier semaphores. Data moves between devices by JAX's collectives and lax.ppermute only.
A program may use at most 128 MiB of HBM per device.

v0:
```python
import jax
import jax.numpy as jnp
from jax import lax
from jax.sharding import PartitionSpec as P

TILE = 8
MAXT = 4


def slot_places(expert_ids, modality, tile_counts, expert):
    capacity = MAXT * TILE
    places = jnp.full(expert_ids.shape, -1, jnp.int32)
    for kind in range(2):
        member = ((expert_ids == expert) & (modality == kind)).astype(jnp.int32)
        rank = jnp.cumsum(member, dtype=jnp.int32) - 1
        limit = tile_counts[kind, expert] * TILE
        keep = (member == 1) & (rank < limit)
        places = jnp.where(keep, kind * capacity + rank, places)
    return places


def slot_table(places):
    slots = lax.broadcasted_iota(jnp.int32, (2 * MAXT * TILE, places.shape[0]), 0)
    return (slots == places[None, :]).astype(jnp.bfloat16)


def place_rows(places, values):
    index = jnp.maximum(places, 0)
    rows = jnp.take(values, index, axis=0)
    return jnp.where((places >= 0)[:, None], rows, jnp.zeros_like(rows))


def per_device(
    tokens,
    expert_ids,
    modality,
    tile_counts,
    router,
    w_gate,
    w_up,
    w_down,
    shared_gate,
    shared_up,
    shared_down,
):
    whole = lax.all_gather(tokens, "row", axis=0, tiled=True)
    expert = lax.axis_index("col")
    places = slot_places(expert_ids, modality, tile_counts, expert)
    table = slot_table(places)
    taken = jnp.dot(table, whole, preferred_element_type=jnp.float32).astype(jnp.bfloat16)
    score = jax.nn.sigmoid(jnp.dot(taken, router, preferred_element_type=jnp.float32))
    scaled = (taken.astype(jnp.float32) * score).astype(jnp.bfloat16)
    gate = jnp.dot(scaled, w_gate[0], preferred_element_type=jnp.float32)
    upper = jnp.dot(scaled, w_up[0], preferred_element_type=jnp.float32)
    hidden = (jax.nn.silu(gate) * upper).astype(jnp.bfloat16)
    result = jnp.dot(hidden, w_down[0], preferred_element_type=jnp.float32)
    width_row = shared_down.shape[1]
    feature_start = lax.axis_index("row") * width_row
    local_rows = lax.dynamic_slice_in_dim(whole, feature_start, width_row, 1)
    gate_part = jnp.dot(local_rows, shared_gate, preferred_element_type=jnp.float32)
    upper_part = jnp.dot(local_rows, shared_up, preferred_element_type=jnp.float32)
    shared_gate_sum, shared_up_sum = lax.psum((gate_part, upper_part), "row")
    shared_hidden = (jax.nn.silu(shared_gate_sum) * shared_up_sum).astype(jnp.bfloat16)
    shared_part = jnp.dot(shared_hidden, shared_down, preferred_element_type=jnp.float32)
    slot_total = lax.psum_scatter(result, "row", scatter_dimension=1, tiled=True)
    combined = place_rows(places, slot_total) + shared_part
    total = lax.psum_scatter(combined, "col", scatter_dimension=0, tiled=True)
    return total.astype(jnp.bfloat16)


def solution(mesh):
    in_specs = (
        P("row", None),
        P(),
        P(),
        P(),
        P(None, "col"),
        P("col", None, "row"),
        P("col", None, "row"),
        P("col", "row", None),
        P("row", "col"),
        P("row", "col"),
        P("col", "row"),
    )
    out_specs = P("col", "row")
    return jax.shard_map(
        per_device, mesh=mesh, in_specs=in_specs, out_specs=out_specs, check_vma=False
    )
```

profile of v0, /device:TPU:0, one launch (start us, length us, event | category | flops | bytes accessed | tf_op | source)
XLA Modules:
  0.0 284.3 jit_solution(9219536786317185767)
XLA Ops:
  6.5 0.0 copy-start
  6.5 0.0 all-gather.2.cloned.1.call-start
  6.5 0.7 all-gather.2.cloned.1.call-update
  7.3 0.0 reduce-scatter.3.cloned.1.call-start
  7.3 1.4 constant_dynamic-slice_fusion.1
  10.0 0.7 convert_bitcast_fusion
  10.7 0.3 reduce-window.24
  11.0 0.1 slice.16
  11.1 0.7 convert_bitcast_fusion.1
  11.8 0.3 reduce-window.16
  12.1 0.1 slice.14
  12.2 0.1 slice_reduce_fusion
  12.3 0.1 broadcast_compare_fusion.1
  12.4 60.8 %all-gather.2.cloned.1.call-done = bf16[512,5120]{1,0:T(8,128)(2,1)} async-done(((bf16[128,5120]{1,0:T(8,128)(2,1)}), bf16[512,5120]{1,0:T(8,128)(2,1)}) %all-gather.2.cloned.1.call-update) | async-done | bytes 5242896 | tf_op jit(solution)/shard_map/all_gather | solution.py:46
  73.2 0.0 copy-start.2
  73.2 3.5 %convolution_convert_fusion = bf16[64,5120]{1,0:T(8,128)(2,1)S(1)} fusion(bf16[512,5120]{1,0:T(8,128)(2,1)} %all-gather.2.cloned.1.call-done, s32[512]{0:T(512)S(1)} %get-tuple-element.8), kind=kOutput, calls=%fused_computation.7 | convolution fusion | flops 335904768 | bytes 5900288 | tf_op jit(solution)/shard_map/dot_general | solution.py:50
  76.8 0.0 copy-done.2
  76.8 0.3 fusion.19
  77.0 6.0 %fusion.4 = f32[64,1024]{1,0:T(8,128)S(1)} fusion(bf16[1,5120,1024]{2,1,0:T(8,128)(2,1)} %param.16, bf16[64,5120]{1,0:T(8,128)(2,1)S(1)} %convolution_convert_fusion, f32[64]{0:T(128)S(1)} %fusion.19), kind=kOutput, calls=%fused_computation.5 | convolution fusion | flops 672071680 | bytes 11403520 | tf_op jit(solution)/shard_map/dot_general | solution.py:53
  83.0 11.9 %fusion = f32[64,5120]{1,0:T(8,128)} fusion(bf16[1,1024,5120]{2,1,0:T(8,128)(2,1)} %param.18, bf16[1,5120,1024]{2,1,0:T(8,128)(2,1)} %param.17, bf16[64,5120]{1,0:T(8,128)(2,1)S(1)} %convolution_convert_fusion, f32[64]{0:T(128)S(1)} %fusion.19, f32[64,1024]{1,0:T(8,128)S(1)} %fusion.4), kind=kOutput, calls=%fused_computation.1 | convolution fusion | flops 1343553536 | bytes 23200000 | tf_op jit(solution)/shard_map/dot_general | solution.py:56
  94.9 0.0 reduce-scatter.3.cloned.1.call-update
  94.9 0.0 all-reduce.3.cloned.1.call-start
  95.0 0.0 copy-start.1
  95.0 5.2 %fusion.9 = f32[512,1024]{1,0:T(8,128)} fusion(bf16[1280,1024]{1,0:T(8,128)(2,1)} %param.20, bf16[512,5120]{1,0:T(8,128)(2,1)} %all-gather.2.cloned.1.call-done, s32[]{:T(128)S(6)} %select_n.29), kind=kOutput, calls=%fused_computation.12 | convolution fusion | flops 1342177280 | bytes 6029316 | tf_op jit(solution)/shard_map/dot_general | solution.py:61
  100.2 0.0 copy-done.1
  100.2 4.2 %fusion.11 = f32[512,1024]{1,0:T(8,128)} fusion(bf16[1280,1024]{1,0:T(8,128)(2,1)S(1)} %copy-done.1, bf16[512,5120]{1,0:T(8,128)(2,1)} %all-gather.2.cloned.1.call-done, s32[]{:T(128)S(6)} %select_n.29), kind=kOutput, calls=%fused_computation.14 | convolution fusion | flops 1342177280 | bytes 6029316 | tf_op jit(solution)/shard_map/dot_general | solution.py:60
  104.4 0.0 all-reduce.3.cloned.1.call-update
  104.5 0.0 reduce-scatter.5.cloned.1.call-start
  104.6 20.0 %reduce-scatter.3.cloned.1.call-done = f32[64,1280]{1,0:T(8,128)} async-done(((f32[64,5120]{1,0:T(8,128)}), f32[64,1280]{1,0:T(8,128)}) %reduce-scatter.3.cloned.1.call-update) | async-done | bytes 327696 | tf_op jit(solution)/shard_map/reduce_scatter | solution.py:65
  124.6 5.0 %gather_fusion = f32[512,1280]{1,0:T(8,128)} fusion(f32[64,1280]{1,0:T(8,128)} %reduce-scatter.3.cloned.1.call-done, s32[1024]{0:T(1024)S(1)} %pad_clamp_fusion), kind=kCustom, calls=%fused_computation | custom fusion | bytes 5244928 | tf_op jit(solution)/shard_map/jit(_take)/gather | solution.py:29
  129.6 102.1 %all-reduce.3.cloned.1.call-done = (f32[512,1024]{1,0:T(8,128)}, f32[512,1024]{1,0:T(8,128)}) async-done(((f32[512,1024]{1,0:T(8,128)}, f32[512,1024]{1,0:T(8,128)}), (f32[512,1024]{1,0:T(8,128)}, f32[512,1024]{1,0:T(8,128)})) %all-reduce.3.cloned.1.call-update) | async-done | bytes 4194320 | tf_op jit(solution)/shard_map/psum | solution.py:62
  231.7 0.0 copy-done
  231.7 6.4 %convolution_add_fusion = f32[512,1280]{1,0:T(8,128)} fusion(bf16[1024,1280]{1,0:T(8,128)(2,1)S(1)} %copy-done, f32[512,1280]{1,0:T(8,128)} %gather_fusion, pred[512]{0:T(512)(128)(4,1)S(1)} %broadcast_compare_fusion, pred[512]{0:T(512)(128)(4,1)S(1)} %get-tuple-element.7, f32[512,1024]{1,0:T(8,128)} %get-tuple-element.5, f32[512,1024]{1,0:T(8,128)} %get-tuple-element.6), kind=kOutput, calls=%fused_computation.8 | convolution fusion | flops 1347289088 | bytes 12059648 | tf_op jit(solution)/shard_map/dot_general | solution.py:64
  238.1 0.0 reduce-scatter.5.cloned.1.call-update
  238.2 38.0 %reduce-scatter.5.cloned.1.call-done = f32[64,1280]{1,0:T(8,128)} async-done(((f32[512,1280]{1,0:T(8,128)}), f32[64,1280]{1,0:T(8,128)}) %reduce-scatter.5.cloned.1.call-update) | async-done | bytes 327696 | tf_op jit(solution)/shard_map/reduce_scatter | solution.py:67
  276.1 1.7 convert_element_type.32
  (5 shorter events, 0.1 us)
Async XLA Ops:
  6.5 225.2 %copy-start = (bf16[1024,1280]{1,0:T(8,128)(2,1)S(1)}, bf16[1024,1280]{1,0:T(8,128)(2,1)}, u32[]{:S(2)}) copy-start(bf16[1024,1280]{1,0:T(8,128)(2,1)} %param.21) | copy-start | bytes 7864324
  6.5 66.7 %all-gather.2.cloned.1.call-start = ((), (), s32[]{:S(2)}) async-start(), calls=%async_computation.2 | async-start | bytes 6553600 | tf_op jit(solution)/shard_map/all_gather | solution.py:46
  7.3 117.3 %reduce-scatter.3.cloned.1.call-start = ((), (), s32[]{:S(2)}) async-start(), calls=%async_computation.3 | async-start | bytes 1638400 | tf_op jit(solution)/shard_map/reduce_scatter | solution.py:65
  73.2 3.5 %copy-start.2 = (bf16[5120,1]{0,1:T(2,128)(2,1)S(1)}, bf16[5120,1]{0,1:T(2,128)(2,1)}, u32[]{:S(2)}) copy-start(bf16[5120,1]{0,1:T(2,128)(2,1)} %param.15) | copy-start | bytes 30724
  94.9 136.8 %all-reduce.3.cloned.1.call-start = ((), (), s32[]{:S(2)}) async-start(), calls=%async_computation.5 | async-start | bytes 8388608 | tf_op jit(solution)/shard_map/psum | solution.py:62
  95.0 5.2 %copy-start.1 = (bf16[1280,1024]{1,0:T(8,128)(2,1)S(1)}, bf16[1280,1024]{1,0:T(8,128)(2,1)}, u32[]{:S(2)}) copy-start(bf16[1280,1024]{1,0:T(8,128)(2,1)} %param.19) | copy-start | bytes 7864324
  104.5 171.7 %reduce-scatter.5.cloned.1.call-start = ((), (), s32[]{:S(2)}) async-start(), calls=%async_computation.4 | async-start | bytes 2949120 | tf_op jit(solution)/shard_map/reduce_scatter | solution.py:67
Sparse Core Ops, SparseCore 0:
  9.2 64.0 all-gather.1
  95.0 29.4 reduce-scatter.2
  128.1 103.5 all-reduce.2
  238.3 37.8 reduce-scatter.4
where the time goes:
time: 285 us; the launch traced here: 284 us
  waiting for transfers between devices  222 us (78%)
  matrix products  37.5 us (13%)
  between operations  14.5 us (5%)
  local copies, waits for them, and re-layouts  6.72 us (2%)
  other arithmetic  3.83 us (1%)
    psum x1, waiting for transfers between devices, per_device(): shared_gate_sum, shared_up_sum = lax.psum((gate_part, upper_part), 'row')  102 us
    all_gather x1, waiting for transfers between devices, per_device(): whole = lax.all_gather(tokens, 'row', axis=0, tiled=True)  60.8 us
    reduce_scatter x1, waiting for transfers between devices, per_device(): total = lax.psum_scatter(combined, 'col', scatter_dimension=0, tiled=True)  38 us
    reduce_scatter x1, waiting for transfers between devices, per_device(): lax.psum_scatter(result, 'row', scatter_dimension=1, tiled=True)  20 us
    dot_general x1, matrix products, per_device(): result = jnp.dot(hidden, w_down[0], preferred_element_type=jnp.float32)  11.9 us
    dot_general x1, matrix products, per_device(): jnp.dot(shared_hidden, shared_down, preferred_element_type=jnp.float32)  6.44 us
    dot_general x1, matrix products, per_device(): gate = jnp.dot(scaled, w_gate[0], preferred_element_type=jnp.float32)  5.99 us
  transfers between devices with their start and end apart: 4, of which 4 were waited for; matrix products, arithmetic and copies ran while one was open for 6% of the time, Pallas kernels for 0%

commit v1 on v0

--- a/solution.py
+++ b/solution.py
@@ -5,6 +5,18 @@
 
 TILE = 8
 MAXT = 4
+
+
+def gather_by_bits(array, axis, dim):
+    ways, here, step = (lax.axis_size(axis), lax.axis_index(axis), array.shape[dim])
+    line, have = (array, 1)
+    while have < ways:
+        line = jnp.concatenate(
+            [line, lax.ppermute(line, axis, [(d, (d - have) % ways) for d in range(ways)])],
+            axis=dim,
+        )
+        have = 2 * have
+    return jnp.roll(line, here * step, axis=dim)
 
 
 def slot_places(expert_ids, modality, tile_counts, expert):
@@ -43,7 +55,7 @@
     shared_up,
     shared_down,
 ):
-    whole = lax.all_gather(tokens, "row", axis=0, tiled=True)
+    whole = gather_by_bits(tokens, "row", 0)
     expert = lax.axis_index("col")
     places = slot_places(expert_ids, modality, tile_counts, expert)
     table = slot_table(places)

time: 285 us -> 316 us (1.11)
  waiting for transfers between devices: 222 us -> 242 us
  local copies, waits for them, and re-layouts: 6.72 us -> 15.9 us
  matrix products: 37.5 us -> 31.2 us
  starting transfers between devices: 0.12 us -> 5.72 us
    ppermute x0 -> x2, waiting for transfers between devices: none -> 80.2 us  [gather_by_bits(): lax.ppermute(line, axis, [(d, (d - have) % ways) for d in range(ways)])]
    all_gather x1 -> x0, waiting for transfers between devices: 60.8 us -> none  [per_device(): whole = lax.all_gather(tokens, 'row', axis=0, tiled=True)]
    unnamed x6 -> x31, local copies, waits for them, and re-layouts: 0.01 us -> 7.88 us
    ppermute x0 -> x2, starting transfers between devices: none -> 5.42 us  [gather_by_bits(): lax.ppermute(line, axis, [(d, (d - have) % ways) for d in range(ways)])]
    dot_general x1, matrix products: 5.99 us -> 2.02 us  [per_device(): gate = jnp.dot(scaled, w_gate[0], preferred_element_type=jnp.float32)]
    concatenate x0 -> x1, other arithmetic: none -> 3.48 us  [gather_by_bits(): jnp.concatenate([line, lax.ppermute(line, axis, [(d, (d - have) % ways) f...]
  transfers between devices with their start and end apart: 4 -> 5, of which waited for: 4 -> 5; matrix products, arithmetic and copies ran while one was open for 6% -> 6% of each run, Pallas kernels for 0% -> 0%
where the time goes in v1:
time: 316 us
  waiting for transfers between devices  242 us (77%)
  matrix products  31.2 us (10%)
  local copies, waits for them, and re-layouts  15.9 us (5%)
  between operations  14.7 us (5%)
  other arithmetic  5.93 us (2%)
  starting transfers between devices  5.72 us (2%)
    psum x1, waiting for transfers between devices, per_device(): shared_gate_sum, shared_up_sum = lax.psum((gate_part, upper_part), 'row')  102 us
    ppermute x2, waiting for transfers between devices, gather_by_bits(): lax.ppermute(line, axis, [(d, (d - have) % ways) for d in range(ways)])  80.2 us
    reduce_scatter x1, waiting for transfers between devices, per_device(): total = lax.psum_scatter(combined, 'col', scatter_dimension=0, tiled=True)  38 us
    reduce_scatter x1, waiting for transfers between devices, per_device(): lax.psum_scatter(result, 'row', scatter_dimension=1, tiled=True)  21.8 us
    dot_general x1, matrix products, per_device(): result = jnp.dot(hidden, w_down[0], preferred_element_type=jnp.float32)  11.9 us
    unnamed x31, local copies, waits for them, and re-layouts  7.88 us
    dot_general x1, matrix products, per_device(): jnp.dot(shared_hidden, shared_down, preferred_element_type=jnp.float32)  6.46 us
  transfers between devices with their start and end apart: 5, of which 5 were waited for; matrix products, arithmetic and copies ran while one was open for 6% of the time, Pallas kernels for 0%

profile of v1, /device:TPU:0, one launch (start us, length us, event | category | flops | bytes accessed | tf_op | source)
XLA Modules:
  0.0 315.6 jit_solution(17590369145521392428)
XLA Ops:
  6.5 0.0 copy-start
  6.5 0.0 reduce-scatter.3.cloned.1.call-start
  6.6 4.0 %collective-permute-start = (bf16[128,5120]{1,0:T(8,128)(2,1)}, bf16[128,5120]{1,0:T(8,128)(2,1)S(1)}, u32[]{:S(2)}, u32[]{:S(2)}) collective-permute-start(bf16[128,5120]{1,0:T(8,128)(2,1)} %param.11), channel_id=1, source_target_pairs={{0,24},{8,0},{16,8},{24,16},{1,25},{9,1},{17,9},{25,17},{2,26},{10... | collective-permute-start | bytes 3932168 | tf_op jit(solution)/shard_map/ppermute | solution.py:15
  10.6 28.4 %collective-permute-done = bf16[128,5120]{1,0:T(8,128)(2,1)S(1)} collective-permute-done((bf16[128,5120]{1,0:T(8,128)(2,1)}, bf16[128,5120]{1,0:T(8,128)(2,1)S(1)}, u32[]{:S(2)}, u32[]{:S(2)}) %collective-permute-start) | collective-permute-done | bytes 1310752 | tf_op jit(solution)/shard_map/ppermute | solution.py:15
  38.9 3.5 %pad_maximum_fusion = bf16[256,5120]{1,0:T(8,128)(2,1)} fusion(bf16[128,5120]{1,0:T(8,128)(2,1)S(1)} %collective-permute-done, bf16[128,5120]{1,0:T(8,128)(2,1)} %param.11), kind=kLoop, calls=%fused_computation.10 | loop fusion | flops 5242880 | bytes 5242880 | tf_op jit(solution)/shard_map/concatenate | solution.py:14
  42.4 0.0 copy-done.2
  42.4 1.4 collective-permute-start.1
  43.8 0.0 copy-done.5
  43.8 0.0 copy-done.6
  43.9 0.3 reduce-window.24
  44.2 0.1 slice.16
  44.3 0.3 reduce-window.16
  44.6 0.1 slice.14
  44.7 0.0 copy-done.7
  44.7 0.7 constant_dynamic-slice_fusion.1
  46.7 0.1 slice_reduce_fusion
  46.9 0.1 broadcast_compare_fusion.1
  47.0 1.5 constant_dynamic-update-slice_fusion.5
  48.5 0.1 constant_dynamic-update-slice_fusion.4
  48.6 0.0 copy-start.1
  48.6 51.9 %collective-permute-done.1 = bf16[256,5120]{1,0:T(8,128)(2,1)} collective-permute-done((bf16[256,5120]{1,0:T(8,128)(2,1)}, bf16[256,5120]{1,0:T(8,128)(2,1)}, u32[]{:S(2)}, u32[]{:S(2)}) %collective-permute-start.1) | collective-permute-done | bytes 2621472 | tf_op jit(solution)/shard_map/ppermute | solution.py:15
  100.5 2.1 constant_dynamic-update-slice_fusion.3
  102.5 0.0 slice-start.1
  102.5 0.1 constant_dynamic-update-slice_fusion.2
  102.6 0.1 constant_dynamic-update-slice_fusion.1
  102.7 0.0 slice-start.2
  102.8 2.1 constant_dynamic-update-slice_fusion
  104.8 0.0 copy-start.4
  104.8 4.0 %copy-done.4 = bf16[1024,5120]{1,0:T(8,128)(2,1)} copy-done((bf16[1024,5120]{1,0:T(8,128)(2,1)}, bf16[1024,5120]{1,0:T(8,128)(2,1)S(1)}, u32[]{:S(2)}) %copy-start.4) | copy-done | bytes 10485784
  108.8 1.0 convolution_convert_fusion
  109.8 0.3 fusion.20
  110.1 0.0 slice-done.1
  110.2 2.0 fusion.4
  112.2 11.9 %fusion = f32[64,5120]{1,0:T(8,128)} fusion(bf16[1,1024,5120]{2,1,0:T(8,128)(2,1)} %param.18, bf16[1,5120,1024]{2,1,0:T(8,128)(2,1)} %param.17, bf16[64,5120]{1,0:T(8,128)(2,1)S(1)} %convolution_convert_fusion, f32[64]{0:T(128)S(1)} %fusion.20, f32[64,1024]{1,0:T(8,128)S(1)} %fusion.4), kind=kOutput, calls=%fused_computation.1 | convolution fusion | flops 1343553536 | bytes 23200000 | tf_op jit(solution)/shard_map/dot_general | solution.py:68
  124.1 0.0 reduce-scatter.3.cloned.1.call-update
  124.1 0.0 all-reduce.3.cloned.1.call-start
  124.2 0.0 copy-start.8
  124.2 5.3 %fusion.10 = f32[512,1024]{1,0:T(8,128)} fusion(bf16[1280,1024]{1,0:T(8,128)(2,1)} %param.20, bf16[1024,5120]{1,0:T(8,128)(2,1)} %copy-done.4, s32[]{:T(128)S(6)} %select_n.48, s32[]{:T(128)S(6)} %select_n.50), kind=kOutput, calls=%fused_computation.14 | convolution fusion | flops 1342177280 | bytes 6029320 | tf_op jit(solution)/shard_map/dot_general | solution.py:73
  129.4 4.3 %fusion.12 = f32[512,1024]{1,0:T(8,128)} fusion(bf16[1280,1024]{1,0:T(8,128)(2,1)S(1)} %copy-done.8, bf16[1024,5120]{1,0:T(8,128)(2,1)} %copy-done.4, s32[]{:T(128)S(6)} %select_n.48, s32[]{:T(128)S(6)} %select_n.50), kind=kOutput, calls=%fused_computation.16 | convolution fusion | flops 1342177280 | bytes 6029320 | tf_op jit(solution)/shard_map/dot_general | solution.py:72
  133.7 0.0 all-reduce.3.cloned.1.call-update
  133.8 0.2 reduce-scatter.5.cloned.1.call-start
  134.0 21.8 %reduce-scatter.3.cloned.1.call-done = f32[64,1280]{1,0:T(8,128)} async-done(((f32[64,5120]{1,0:T(8,128)}), f32[64,1280]{1,0:T(8,128)}) %reduce-scatter.3.cloned.1.call-update) | async-done | bytes 327696 | tf_op jit(solution)/shard_map/reduce_scatter | solution.py:77
  155.8 5.0 %gather_fusion = f32[512,1280]{1,0:T(8,128)} fusion(f32[64,1280]{1,0:T(8,128)} %reduce-scatter.3.cloned.1.call-done, s32[1024]{0:T(1024)S(1)} %pad_clamp_fusion), kind=kCustom, calls=%fused_computation | custom fusion | bytes 5244928 | tf_op jit(solution)/shard_map/jit(_take)/gather | solution.py:41
  160.8 102.1 %all-reduce.3.cloned.1.call-done = (f32[512,1024]{1,0:T(8,128)}, f32[512,1024]{1,0:T(8,128)}) async-done(((f32[512,1024]{1,0:T(8,128)}, f32[512,1024]{1,0:T(8,128)}), (f32[512,1024]{1,0:T(8,128)}, f32[512,1024]{1,0:T(8,128)})) %all-reduce.3.cloned.1.call-update) | async-done | bytes 4194320 | tf_op jit(solution)/shard_map/psum | solution.py:74
  262.9 6.5 %convolution_add_fusion = f32[512,1280]{1,0:T(8,128)} fusion(bf16[1024,1280]{1,0:T(8,128)(2,1)S(1)} %copy-done, f32[512,1280]{1,0:T(8,128)} %gather_fusion, pred[512]{0:T(512)(128)(4,1)S(1)} %broadcast_compare_fusion, pred[512]{0:T(512)(128)(4,1)S(1)} %get-tuple-element.7, f32[512,1024]{1,0:T(8,128)} %get-tuple-element.5, f32[512,1024]{1,0:T(8,128)} %get-tuple-element.6), kind=kOutput, calls=%fused_computation.9 | convolution fusion | flops 1347289088 | bytes 12059648 | tf_op jit(solution)/shard_map/dot_general | solution.py:76
  269.4 0.0 reduce-scatter.5.cloned.1.call-update
  269.4 38.0 %reduce-scatter.5.cloned.1.call-done = f32[64,1280]{1,0:T(8,128)} async-done(((f32[512,1280]{1,0:T(8,128)}), f32[64,1280]{1,0:T(8,128)}) %reduce-scatter.5.cloned.1.call-update) | async-done | bytes 327696 | tf_op jit(solution)/shard_map/reduce_scatter | solution.py:79
  307.4 1.7 convert_element_type.32
  (22 shorter events, 0.1 us)
Async XLA Ops:
  6.5 256.4 %copy-start = (bf16[1024,1280]{1,0:T(8,128)(2,1)S(1)}, bf16[1024,1280]{1,0:T(8,128)(2,1)}, u32[]{:S(2)}) copy-start(bf16[1024,1280]{1,0:T(8,128)(2,1)} %param.21) | copy-start | bytes 7864324
  6.5 37.3 %copy-start.5 = (s32[512]{0:T(512)S(1)}, s32[512]{0:T(512)}, u32[]{:S(2)}) copy-start(s32[512]{0:T(512)} %param.13) | copy-start | bytes 6148
  6.5 37.3 %copy-start.6 = (s32[512]{0:T(512)S(1)}, s32[512]{0:T(512)}, u32[]{:S(2)}) copy-start(s32[512]{0:T(512)} %param.12) | copy-start | bytes 6148
  6.5 38.2 %copy-start.7 = (s32[2,8]{1,0:T(2,128)S(1)}, s32[2,8]{1,0:T(2,128)}, u32[]{:S(2)}) copy-start(s32[2,8]{1,0:T(2,128)} %param.14) | copy-start | bytes 196
  6.5 149.2 %reduce-scatter.3.cloned.1.call-start = ((), (), s32[]{:S(2)}) async-start(), calls=%async_computation.2 | async-start | bytes 1638400 | tf_op jit(solution)/shard_map/reduce_scatter | solution.py:77
  6.6 32.3 %collective-permute-start = (bf16[128,5120]{1,0:T(8,128)(2,1)}, bf16[128,5120]{1,0:T(8,128)(2,1)S(1)}, u32[]{:S(2)}, u32[]{:S(2)}) collective-permute-start(bf16[128,5120]{1,0:T(8,128)(2,1)} %param.11), channel_id=1, source_target_pairs={{0,24},{8,0},{16,8},{24,16},{1,25},{9,1},{17,9},{25,17},{2,26},{10... | collective-permute-start | bytes 3932168 | tf_op jit(solution)/shard_map/ppermute | solution.py:15
  38.9 3.5 %copy-start.2 = (bf16[128,5120]{1,0:T(8,128)(2,1)}, bf16[128,5120]{1,0:T(8,128)(2,1)S(1)}, u32[]{:S(2)}) copy-start(bf16[128,5120]{1,0:T(8,128)(2,1)S(1)} %collective-permute-done) | copy-start | bytes 3932164
  42.4 58.1 %collective-permute-start.1 = (bf16[256,5120]{1,0:T(8,128)(2,1)}, bf16[256,5120]{1,0:T(8,128)(2,1)}, u32[]{:S(2)}, u32[]{:S(2)}) collective-permute-start(bf16[256,5120]{1,0:T(8,128)(2,1)} %pad_maximum_fusion), channel_id=1, source_target_pairs={{0,16},{8,24},{16,0},{24,8},{1,17},{9,25},{17,1},{25,9},{2,18},{10... | collective-permute-start | bytes 7864328 | tf_op jit(solution)/shard_map/ppermute | solution.py:15
  46.7 1.8 copy-start.3
  48.6 53.9 %copy-start.1 = (bf16[128,5120]{1,0:T(8,128)(2,1)S(1)}, bf16[128,5120]{1,0:T(8,128)(2,1)}, u32[]{:S(2)}) copy-start(bf16[128,5120]{1,0:T(8,128)(2,1)} %param.11) | copy-start | bytes 3932164
  100.5 9.6 %slice-start = ((s8[10485760]{0:T(1024)(128)(4,1)}), s8[4194304]{0:T(1024)(128)(4,1)S(1)}, s32[]{:S(2)}) async-start(s8[10485760]{0:T(1024)(128)(4,1)} %bitcast.56), calls=%async_computation.5 | async-start | bytes 8388608
  102.5 7.6 %slice-start.1 = ((s8[10485760]{0:T(1024)(128)(4,1)}), s8[4194304]{0:T(1024)(128)(4,1)S(1)}, s32[]{:S(2)}) async-start(s8[10485760]{0:T(1024)(128)(4,1)} %bitcast.56), calls=%async_computation.6 | async-start | bytes 8388608
  102.7 7.4 %slice-start.2 = ((s8[10485760]{0:T(1024)(128)(4,1)}), s8[2097152]{0:T(1024)(128)(4,1)S(1)}, s32[]{:S(2)}) async-start(s8[10485760]{0:T(1024)(128)(4,1)} %bitcast.56), calls=%async_computation.7 | async-start | bytes 4194304
  104.8 4.0 %copy-start.4 = (bf16[1024,5120]{1,0:T(8,128)(2,1)}, bf16[1024,5120]{1,0:T(8,128)(2,1)S(1)}, u32[]{:S(2)}) copy-start(bf16[1024,5120]{1,0:T(8,128)(2,1)S(1)} %constant_dynamic-update-slice_fusion) | copy-start | bytes 31457284
  108.8 1.0 copy-start.9
  124.1 138.8 %all-reduce.3.cloned.1.call-start = ((), (), s32[]{:S(2)}) async-start(), calls=%async_computation.4 | async-start | bytes 8388608 | tf_op jit(solution)/shard_map/psum | solution.py:74
  124.2 5.3 %copy-start.8 = (bf16[1280,1024]{1,0:T(8,128)(2,1)S(1)}, bf16[1280,1024]{1,0:T(8,128)(2,1)}, u32[]{:S(2)}) copy-start(bf16[1280,1024]{1,0:T(8,128)(2,1)} %param.19) | copy-start | bytes 7864324
  133.8 173.6 %reduce-scatter.5.cloned.1.call-start = ((), (), s32[]{:S(2)}) async-start(), calls=%async_computation.3 | async-start | bytes 2949120 | tf_op jit(solution)/shard_map/reduce_scatter | solution.py:79
Sparse Core Ops, SparseCore 0:
  124.2 31.5 reduce-scatter.2
  159.3 103.5 all-reduce.2
  269.5 37.8 reduce-scatter.4
